TPU v7x, 32 devices: a whole 2x2x4 slice. The times are simulated.
32 devices in a mesh: rep: 1, ep: 32 (over z, y, x, core).
Axes of the slice: x: 2, y: 2, z: 4, core: 2. Of those that a mesh axis runs over, the one named last changes fastest.
Arguments:
- tokens: bfloat16 [512, 3584], P(('rep', 'ep')), may hold values from -6 to 6
- routes: int32 [512, 8], P(('rep', 'ep')), may hold values from 0 to 15, all different within a row; in each aligned block of 16 rows (0 to 15, 16 to 31, ...) at most 16 rows name the same one
- gate_weights: float32 [512, 8], P(('rep', 'ep')), may hold values from 0.05 to 0.5
- w_gate: bfloat16 [32, 3584, 512], P('ep'), may hold values from -0.09375 to 0.09375
- w_up: bfloat16 [32, 3584, 512], P('ep'), may hold values from -0.09375 to 0.09375
- w_down: bfloat16 [32, 512, 3584], P('ep'), may hold values from -0.1875 to 0.1875
Outputs:
- mixed: bfloat16 [512, 3584], P(('rep', 'ep'))
Inputs may be any that keep to these rules, and one draw needn't show every extreme that they name: `routes`: each token names 8 different experts. Among the tokens of one device at most 16 name any one expert, and in every draw some expert is named by exactly 16 tokens of some device.
All inputs are finite; a program needn't handle non-finite values.
Results may differ from a plain program's by a relative error of at most 0.008.
Values may be sent and summed in bfloat16 or wider, within the bound.
No kernel may reach another device: no remote copies, remote signals or barrier semaphores. Data moves between devices by JAX's collectives and lax.ppermute only.
A program may use at most 128 MiB of HBM per device.

v0:
```python
import jax
import jax.numpy as jnp
from jax import lax
from jax.sharding import PartitionSpec as P


def swapped(value, axis, bit):
    mask = 2**bit
    pairs = [(source, source ^ mask) for source in range(lax.axis_size(axis))]
    return lax.ppermute(value, axis, pairs)


def slot_positions(chosen, expert_count):
    chosen_hits = jnp.sum(
        (chosen[:, :, None] == jnp.arange(expert_count, dtype=jnp.int32)[None, None, :]).astype(
            jnp.int32
        ),
        axis=1,
        dtype=jnp.int32,
    )
    before = jnp.cumsum(chosen_hits, axis=0, dtype=jnp.int32) - chosen_hits
    return jnp.take_along_axis(before, chosen, axis=1)


def expert_half(expert_rows, w_gate, w_up, w_down):
    gate_value = jnp.dot(expert_rows, w_gate[0], preferred_element_type=jnp.float32)
    up_value = jnp.dot(expert_rows, w_up[0], preferred_element_type=jnp.float32)
    hidden = (jax.nn.silu(gate_value) * up_value).astype(jnp.bfloat16)
    return jnp.dot(hidden, w_down[0], preferred_element_type=jnp.float32).astype(jnp.bfloat16)


def body(tokens, routes, gate_weights, w_gate, w_up, w_down):
    row_count = tokens.shape[0]
    top_count = routes.shape[1]
    width = tokens.shape[1]
    devices = lax.axis_size("ep")
    expert_count = devices // 2
    capacity = min(row_count, 2 * row_count * top_count // expert_count)
    half_cap = capacity // 2
    parity = lax.axis_index("ep") % 2
    slot_index = slot_positions(routes, expert_count)
    flat_index = (routes * capacity + slot_index).reshape(-1)
    buffer = (
        jnp.zeros((expert_count * capacity, width), jnp.bfloat16)
        .at[flat_index]
        .set(jnp.repeat(tokens, top_count, axis=0))
    )
    buffer = buffer.reshape(expert_count, capacity, width)
    outgoing = buffer.reshape(devices, half_cap, width)
    own_half = lax.all_to_all(outgoing, "ep", split_axis=0, concat_axis=0, tiled=True)
    partner_half = swapped(own_half, "ep", 0)
    lower_half = jnp.where(parity == 0, own_half, partner_half)
    upper_half = jnp.where(parity == 0, partner_half, own_half)
    arrived = jnp.concatenate([lower_half, upper_half], axis=1)
    expert_rows = arrived.reshape(devices * capacity, width)
    partial_value = expert_half(expert_rows, w_gate, w_up, w_down).reshape(devices, capacity, width)
    returned = lax.all_to_all(partial_value, "ep", split_axis=0, concat_axis=0, tiled=True)
    paired = returned.reshape(expert_count, 2, capacity, width)
    expert_out = (paired[:, 0].astype(jnp.float32) + paired[:, 1].astype(jnp.float32)).astype(
        jnp.bfloat16
    )
    table = expert_out.reshape(expert_count * capacity, width)
    picked = table[flat_index].reshape(row_count, top_count, width).astype(jnp.float32)
    mixed = jnp.einsum("tk,tkd->td", gate_weights, picked)
    return mixed.astype(jnp.bfloat16)


def solution(mesh):
    placed = (
        P(("rep", "ep"), None),
        P(("rep", "ep"), None),
        P(("rep", "ep"), None),
        P("ep", None, None),
        P("ep", None, None),
        P("ep", None, None),
    )
    return jax.shard_map(
        body, mesh=mesh, in_specs=placed, out_specs=P(("rep", "ep"), None), check_vma=False
    )
```

profile of v0, /device:TPU:0, one launch (start us, length us, event | category | flops | bytes accessed | tf_op | source)
XLA Modules:
  0.0 168.6 jit_solution(2942011848193091434)
XLA Ops:
  0.0 0.0 copy-start
  0.0 0.8 copy.19
  0.8 0.7 bitcast_or_fusion
  1.5 0.1 convert_reduce_fusion
  1.6 0.1 copy.20
  1.7 0.1 reshape.78
  1.8 0.0 copy-start.2
  1.8 1.3 gather_fusion.1
  3.1 0.1 reshape.81
  3.2 0.1 copy.21
  3.2 0.0 copy-done.2
  3.2 0.1 copy.22
  3.3 0.1 reshape.64
  3.4 2.5 %scatter_custom_fusion = bf16[256,3584]{1,0:T(8,128)(2,1)S(1)} fusion(s32[128]{0:T(128)S(1)} %fusion.16, bf16[]{:T(256)} %constant.39.clone.1, bf16[16,3584]{1,0:T(8,128)(2,1)S(1)} %copy-done), kind=kCustom, calls=%fused_computation.18 | custom fusion | bytes 1949698 | tf_op jit(solution)/shard_map/scatter | solution.py:46
  5.9 50.3 %all_to_all.10 = bf16[32,8,3584]{2,1,0:T(8,128)(2,1)} all-to-all(bf16[32,8,3584]{2,1,0:T(8,128)(2,1)S(1)} %bitcast.46), channel_id=1, replica_groups=mesh['rep'=1,'ep'=32] {'ep'}, dimensions={0} | all-to-all | bytes 3670016 | tf_op jit(solution)/shard_map/all_to_all | solution.py:50
  56.2 0.0 collective-permute-start
  56.2 4.0 %collective-permute-done = bf16[32,8,3584]{2,1,0:T(8,128)(2,1)S(1)} collective-permute-done((bf16[32,8,3584]{2,1,0:T(8,128)(2,1)}, bf16[32,8,3584]{2,1,0:T(8,128)(2,1)S(1)}, u32[]{:S(2)}, u32[]{:S(2)}) %collective-permute-start) | collective-permute-done | bytes 1835040 | tf_op jit(solution)/shard_map/ppermute | solution.py:10
  60.2 1.7 %broadcast_select_fusion.1 = (bf16[32,8,3584]{2,1,0:T(8,128)(2,1)S(1)}, bf16[32,8,3584]{2,1,0:T(8,128)(2,1)S(1)}) fusion(bf16[32,8,3584]{2,1,0:T(8,128)(2,1)} %all_to_all.10, bf16[32,8,3584]{2,1,0:T(8,128)(2,1)S(1)} %collective-permute-done, pred[]{:T(512)S(6)} %eq.10), kind=kLoop, calls=%fused_computation.14 | loop fusion | flops 1835008 | bytes 7340033 | tf_op jit(solution)/shard_map/jit(_where)/select_n | solution.py:52
  62.0 0.0 copy-start.4
  62.0 0.5 pad_maximum_fusion
  62.5 1.9 %copy-done.1 = bf16[32,16,3584]{2,1,0:T(8,128)(2,1)} copy-done((bf16[32,16,3584]{2,1,0:T(8,128)(2,1)}, bf16[32,16,3584]{2,1,0:T(8,128)(2,1)S(1)}, u32[]{:S(2)}) %copy-start.1) | copy-done | bytes 3670040
  64.3 1.0 copy-done.4
  65.3 2.0 %fusion.1 = f32[512,512]{1,0:T(8,128)S(1)} fusion(bf16[512,3584]{1,0:T(8,128)(2,1)S(1)} %bitcast.48, bf16[1,3584,512]{2,1,0:T(8,128)(2,1)S(1)} %copy-done.4), kind=kOutput, calls=%fused_computation.6 | convolution fusion | flops 1879048192 | bytes 8388608 | tf_op jit(solution)/shard_map/dot_general | solution.py:27
  67.4 10.1 %convolution_convert_fusion = bf16[512,3584]{1,0:T(8,128)(2,1)} fusion(bf16[1,512,3584]{2,1,0:T(8,128)(2,1)} %param.11, f32[512,512]{1,0:T(8,128)S(1)} %fusion.1, bf16[512,3584]{1,0:T(8,128)(2,1)} %bitcast.49, bf16[1,3584,512]{2,1,0:T(8,128)(2,1)} %param.9), kind=kOutput, calls=%fused_computation.3 | convolution fusion | flops 3761504256 | bytes 15728640 | tf_op jit(solution)/shard_map/dot_general | solution.py:29
  77.5 3.7 %all-to-all-start.1 = ((bf16[32,16,3584]{2,1,0:T(8,128)(2,1)}), bf16[32,16,3584]{2,1,0:T(8,128)(2,1)}, u32[]{:S(2)}, u32[]{:S(2)}) async-start(bf16[32,16,3584]{2,1,0:T(8,128)(2,1)} %bitcast.47), calls=%async_computation.1 | async-start | bytes 7340032 | tf_op jit(solution)/shard_map/all_to_all | solution.py:57
  81.2 0.0 copy-done.3
  81.3 0.1 copy.25
  81.3 82.4 %all-to-all-done.1 = bf16[32,16,3584]{2,1,0:T(8,128)(2,1)} async-done(((bf16[32,16,3584]{2,1,0:T(8,128)(2,1)}), bf16[32,16,3584]{2,1,0:T(8,128)(2,1)}, u32[]{:S(2)}, u32[]{:S(2)}) %all-to-all-start.1) | async-done | bytes 3670048 | tf_op jit(solution)/shard_map/all_to_all | solution.py:57
  163.8 2.6 %add_convert_fusion = bf16[16,1,16,3584]{3,2,0,1:T(8,128)(2,1)S(1)} fusion(bf16[16,2,16,3584]{3,2,1,0:T(8,128)(2,1)} %bitcast.9), kind=kLoop, calls=%fused_computation.10 | loop fusion | flops 3670016 | bytes 5505024 | tf_op jit(solution)/shard_map/convert_element_type | solution.py:59
  166.4 1.1 gather_fusion
  167.5 0.4 fusion.5
  167.9 0.7 copy.30
  (8 shorter events, 0.1 us)
Async XLA Ops:
  0.0 3.4 %copy-start = (bf16[16,3584]{1,0:T(8,128)(2,1)S(1)}, bf16[16,3584]{1,0:T(8,128)(2,1)}, u32[]{:S(2)}) copy-start(bf16[16,3584]{1,0:T(8,128)(2,1)} %param.6) | copy-start | bytes 344068
  1.8 1.4 copy-start.2
  56.2 4.0 %collective-permute-start = (bf16[32,8,3584]{2,1,0:T(8,128)(2,1)}, bf16[32,8,3584]{2,1,0:T(8,128)(2,1)S(1)}, u32[]{:S(2)}, u32[]{:S(2)}) collective-permute-start(bf16[32,8,3584]{2,1,0:T(8,128)(2,1)} %all_to_all.10), channel_id=1, source_target_pairs={{0,1},{1,0},{2,3},{3,2},{4,5},{5,4},{6,7},{7,6},{8,9},{9,8},{10,11... | collective-permute-start | bytes 5505032 | tf_op jit(solution)/shard_map/ppermute | solution.py:10
  62.0 3.4 %copy-start.4 = (bf16[1,3584,512]{2,1,0:T(8,128)(2,1)S(1)}, bf16[1,3584,512]{2,1,0:T(8,128)(2,1)}, u32[]{:S(2)}) copy-start(bf16[1,3584,512]{2,1,0:T(8,128)(2,1)} %param.10) | copy-start | bytes 11010052
  62.5 1.9 %copy-start.1 = (bf16[32,16,3584]{2,1,0:T(8,128)(2,1)}, bf16[32,16,3584]{2,1,0:T(8,128)(2,1)S(1)}, u32[]{:S(2)}) copy-start(bf16[32,16,3584]{2,1,0:T(8,128)(2,1)S(1)} %pad_maximum_fusion) | copy-start | bytes 11010052
  77.5 3.7 %copy-start.3 = (f32[16,8]{0,1:T(8,128)S(1)}, f32[16,8]{0,1:T(8,128)}, u32[]{:S(2)}) copy-start(f32[16,8]{0,1:T(8,128)} %param.8) | copy-start | bytes 1540
  77.5 86.3 %all-to-all-start.1 = ((bf16[32,16,3584]{2,1,0:T(8,128)(2,1)}), bf16[32,16,3584]{2,1,0:T(8,128)(2,1)}, u32[]{:S(2)}, u32[]{:S(2)}) async-start(bf16[32,16,3584]{2,1,0:T(8,128)(2,1)} %bitcast.47), calls=%async_computation.1 | async-start | bytes 7340032 | tf_op jit(solution)/shard_map/all_to_all | solution.py:57
where the time goes:
time: 169 us
  waiting for transfers between devices  86.4 us (51%)
  blocking collectives  50.3 us (30%)
  matrix products  12.6 us (7%)
  local copies, waits for them, and re-layouts  9.75 us (6%)
  other arithmetic  5.7 us (3%)
  starting transfers between devices  3.74 us (2%)
    all_to_all x1, waiting for transfers between devices, body(): lax.all_to_all(partial_value, 'ep', split_axis=0, concat_axis=0, tiled=True)  82.4 us
    all_to_all x1, blocking collectives, body(): lax.all_to_all(outgoing, 'ep', split_axis=0, concat_axis=0, tiled=True)  50.3 us
    dot_general x1, matrix products, expert_half(): jnp.dot(hidden, w_down[0], preferred_element_type=jnp.float32)  10.1 us
    ppermute x1, waiting for transfers between devices, swapped(): return lax.ppermute(value, axis, pairs)  3.99 us
    unnamed x12, local copies, waits for them, and re-layouts  3.75 us
    all_to_all x1, starting transfers between devices, body(): lax.all_to_all(partial_value, 'ep', split_axis=0, concat_axis=0, tiled=True)  3.73 us
  transfers between devices with their start and end apart: 2, of which 2 were waited for; matrix products, arithmetic and copies ran while one was open for 0% of the time, Pallas kernels for 0%

commit v1 on v0

v1 whole, which is shorter than its diff:
```python
import jax
import jax.numpy as jnp
from jax import lax
from jax.sharding import PartitionSpec as P


def dense_gates(routes, gate_weights, expert_count):
    hits = routes[:, :, None] == jnp.arange(expert_count, dtype=jnp.int32)[None, None, :]
    return jnp.sum(jnp.where(hits, gate_weights[:, :, None], 0.0), axis=1)


def body(tokens, routes, gate_weights, w_gate, w_up, w_down):
    devices = lax.axis_size("ep")
    expert = lax.axis_index("ep") // 2
    gates = dense_gates(routes, gate_weights, devices // 2)
    all_gates = lax.all_gather(gates, "ep", axis=0, tiled=True)
    rows = lax.all_gather(tokens, "ep", axis=0, tiled=True)
    gate_value = jnp.dot(rows, w_gate[0], preferred_element_type=jnp.float32)
    up_value = jnp.dot(rows, w_up[0], preferred_element_type=jnp.float32)
    hidden = (jax.nn.silu(gate_value) * up_value).astype(jnp.bfloat16)
    partial_value = jnp.dot(hidden, w_down[0], preferred_element_type=jnp.float32)
    mine = jnp.arange(devices // 2, dtype=jnp.int32) == expert
    weight = jnp.sum(jnp.where(mine[None, :], all_gates, 0.0), axis=1)
    weighted = (partial_value * weight[:, None]).astype(jnp.bfloat16)
    return lax.psum_scatter(weighted, "ep", scatter_dimension=0, tiled=True)


def solution(mesh):
    placed = (
        P(("rep", "ep"), None),
        P(("rep", "ep"), None),
        P(("rep", "ep"), None),
        P("ep", None, None),
        P("ep", None, None),
        P("ep", None, None),
    )
    return jax.shard_map(
        body, mesh=mesh, in_specs=placed, out_specs=P(("rep", "ep"), None), check_vma=False
    )
```

time: 169 us -> 236 us (1.40)
  waiting for transfers between devices: 86.4 us -> 161 us
  between operations: 0.14 us -> 13.4 us
  local copies, waits for them, and re-layouts: 9.75 us -> 1.52 us
  blocking collectives: 50.3 us -> 44.3 us
  other arithmetic: 5.7 us -> 0.26 us
  starting transfers between devices: 3.74 us -> 0.04 us
  matrix products: 12.6 us -> 15.3 us
    reduce_scatter x0 -> x1, waiting for transfers between devices: none -> 140 us  [body(): return lax.psum_scatter(weighted, 'ep', scatter_dimension=0, tiled=True)]
    all_to_all x1 -> x0, waiting for transfers between devices: 82.4 us -> none  [body(): lax.all_to_all(partial_value, 'ep', split_axis=0, concat_axis=0, tiled=True)]
    all_to_all x1 -> x0, blocking collectives: 50.3 us -> none  [body(): lax.all_to_all(outgoing, 'ep', split_axis=0, concat_axis=0, tiled=True)]
    all_gather x0 -> x1, blocking collectives: none -> 44.3 us  [body(): all_gates = lax.all_gather(gates, 'ep', axis=0, tiled=True)]
    all_gather x0 -> x1, waiting for transfers between devices: none -> 20 us  [body(): rows = lax.all_gather(tokens, 'ep', axis=0, tiled=True)]
    ppermute x1 -> x0, waiting for transfers between devices: 3.99 us -> none  [swapped(): return lax.ppermute(value, axis, pairs)]
    all_to_all x1 -> x0, starting transfers between devices: 3.73 us -> none  [body(): lax.all_to_all(partial_value, 'ep', split_axis=0, concat_axis=0, tiled=True)]
    dot_general x3 -> x2, matrix products: 12.6 us -> 15.3 us  [the longest x1 10.1 us: body(): jnp.dot(hidden, w_down[0], preferred_element_type=jnp.float32)]
  transfers between devices with their start and end apart: 2 -> 2, of which waited for: 2 -> 2; matrix products, arithmetic and copies ran while one was open for 0% -> 1% of each run, Pallas kernels for 0% -> 0%
where the time goes in v1:
time: 236 us
  waiting for transfers between devices  161 us (68%)
  blocking collectives  44.3 us (19%)
  matrix products  15.3 us (6%)
  between operations  13.4 us (6%)
    reduce_scatter x1, waiting for transfers between devices, body(): return lax.psum_scatter(weighted, 'ep', scatter_dimension=0, tiled=True)  140 us
    all_gather x1, blocking collectives, body(): all_gates = lax.all_gather(gates, 'ep', axis=0, tiled=True)  44.3 us
    all_gather x1, waiting for transfers between devices, body(): rows = lax.all_gather(tokens, 'ep', axis=0, tiled=True)  20 us
    dot_general x1, matrix products, body(): jnp.dot(hidden, w_down[0], preferred_element_type=jnp.float32)  10.1 us
    dot_general x1, matrix products, body(): gate_value = jnp.dot(rows, w_gate[0], preferred_element_type=jnp.float32)  5.21 us
  transfers between devices with their start and end apart: 2, of which 2 were waited for; matrix products, arithmetic and copies ran while one was open for 1% of the time, Pallas kernels for 0%

profile of v1, /device:TPU:0, one launch (start us, length us, event | category | flops | bytes accessed | tf_op | source)
XLA Modules:
  0.0 235.9 jit_solution(8553971272255911643)
XLA Ops:
  6.5 0.0 all-gather.2.cloned.1.call-start
  6.5 0.7 all-gather.2.cloned.1.call-update
  7.3 0.0 reduce-scatter.2.cloned.1.call-start
  7.3 0.8 copy.9
  8.1 0.8 copy.10
  8.8 0.1 select_reduce_fusion.1
  8.9 44.3 %all_gather.7 = f32[512,16]{1,0:T(8,128)S(1)} all-gather(f32[16,16]{1,0:T(8,128)S(1)} %select_reduce_fusion.1), channel_id=1, replica_groups=mesh['rep'=1,'ep'=32] {'ep'}, dimensions={0}, use_global_device_ids=true | all-gather | bytes 33792 | tf_op jit(solution)/shard_map/all_gather | solution.py:16
  53.2 0.1 select_reduce_fusion
  53.4 20.0 %all-gather.2.cloned.1.call-done = bf16[512,3584]{1,0:T(8,128)(2,1)} async-done(((bf16[16,3584]{1,0:T(8,128)(2,1)}), bf16[512,3584]{1,0:T(8,128)(2,1)}) %all-gather.2.cloned.1.call-update) | async-done | bytes 3670032 | tf_op jit(solution)/shard_map/all_gather | solution.py:17
  73.4 5.2 %fusion.3 = f32[512,512]{1,0:T(8,128)S(1)} fusion(bf16[512,3584]{1,0:T(8,128)(2,1)} %all-gather.2.cloned.1.call-done, bf16[1,3584,512]{2,1,0:T(8,128)(2,1)} %param.9), kind=kOutput, calls=%fused_computation.4 | convolution fusion | flops 1879048192 | bytes 8388608 | tf_op jit(solution)/shard_map/dot_general | solution.py:18
  78.6 10.1 %multiply_convert_fusion = bf16[512,3584]{1,0:T(8,128)(2,1)} fusion(bf16[1,512,3584]{2,1,0:T(8,128)(2,1)} %param.11, f32[512]{0:T(512)S(1)} %select_reduce_fusion, bf16[512,3584]{1,0:T(8,128)(2,1)} %all-gather.2.cloned.1.call-done, bf16[1,3584,512]{2,1,0:T(8,128)(2,1)} %param.10, f32[512,512]{1,0:T(8,128)S(1)} %fusion.3), kind=kOutput, calls=%fused_computation | convolution fusion | flops 3763339264 | bytes 15730688 | tf_op jit(solution)/shard_map/dot_general | solution.py:21
  88.7 0.0 reduce-scatter.2.cloned.1.call-update
  88.7 140.3 %reduce-scatter.2.cloned.1.call-done = bf16[16,3584]{1,0:T(8,128)(2,1)} async-done(((bf16[512,3584]{1,0:T(8,128)(2,1)}), bf16[16,3584]{1,0:T(8,128)(2,1)}) %reduce-scatter.2.cloned.1.call-update) | async-done | bytes 114704 | tf_op jit(solution)/shard_map/reduce_scatter | solution.py:25
  (1 shorter events, 0.0 us)
Async XLA Ops:
  6.5 66.9 %all-gather.2.cloned.1.call-start = ((), (), s32[]{:S(2)}) async-start(), calls=%async_computation.1 | async-start | bytes 3784704 | tf_op jit(solution)/shard_map/all_gather | solution.py:17
  7.3 221.8 %reduce-scatter.2.cloned.1.call-start = ((), (), s32[]{:S(2)}) async-start(), calls=%async_computation.2 | async-start | bytes 3784704 | tf_op jit(solution)/shard_map/reduce_scatter | solution.py:25
Sparse Core Ops, SparseCore 0:
  10.2 63.1 all-gather.1
  88.9 140.1 reduce-scatter.1

commit v2 on v1

v2 whole, which is shorter than its diff:
```python
import jax
import jax.numpy as jnp
from jax import lax
from jax.sharding import PartitionSpec as P


def exchange(value, mask):
    pairs = [(source, source ^ mask) for source in range(lax.axis_size("ep"))]
    return lax.ppermute(value, "ep", pairs)


def tree_plan(bits):
    steps = []
    for hops in range(1, bits):
        chosen = {bit: [] for bit in range(bits)}
        for mask in range(1 << bits):
            if mask.bit_count() == hops:
                held = [bit for bit in range(bits) if mask >> bit & 1]
                bit = min(held, key=lambda candidate: len(chosen[candidate]))
                chosen[bit].append(mask)
        steps.append([(bit, masks) for bit, masks in chosen.items() if masks])
    return steps


def joined(parts):
    return parts[0] if len(parts) == 1 else jnp.concatenate(parts, axis=0)


def gather_rows(own, bits):
    count = own.shape[0]
    held = {0: jnp.concatenate([own, exchange(own, 2 << bits)], axis=0)}
    for step in tree_plan(bits):
        for bit, masks in step:
            arrived = exchange(joined([held[mask ^ (1 << bit)] for mask in masks]), 2 << bit)
            for place, mask in enumerate(masks):
                held[mask] = arrived[2 * count * place : 2 * count * (place + 1)]
    last = (1 << bits) - 1
    halves = [
        exchange(held[last ^ (1 << bit)][bit * count : (bit + 1) * count], 2 << bit)
        for bit in range(2)
    ]
    held[last] = jnp.concatenate(halves, axis=0)
    return held


def added(left, right):
    return (left.astype(jnp.float32) + right.astype(jnp.float32)).astype(left.dtype)


def reduce_rows(held, bits):
    last = (1 << bits) - 1
    count = held[last].shape[0] // 2
    extra = {}
    for bit in range(2):
        rows = slice(bit * count, (bit + 1) * count)
        arrived = exchange(held[last][rows], 2 << bit)
        mask = last ^ (1 << bit)
        halves = [held[mask][:count], held[mask][count:]]
        halves[bit] = added(halves[bit], arrived)
        extra[mask] = jnp.concatenate(halves, axis=0)
    held = {**held, **extra}
    for step in reversed(tree_plan(bits)):
        for bit, masks in step:
            arrived = exchange(joined([held[mask] for mask in masks]), 2 << bit)
            for place, mask in enumerate(masks):
                target = mask ^ (1 << bit)
                piece = arrived[2 * count * place : 2 * count * (place + 1)]
                held[target] = added(held[target], piece)
    arrived = exchange(held[0][count:], 2 << bits)
    return added(held[0][:count], arrived)


def gate_columns(routes, gate_weights, expert_count):
    hits = routes[:, :, None] == jnp.arange(expert_count, dtype=jnp.int32)[None, None, :]
    left = jnp.sum(jnp.where(hits, gate_weights[:, :, None], 0.0), axis=1)
    pieces = []
    for _ in range(3):
        piece = lax.reduce_precision(left, 8, 7)
        pieces.append(piece.astype(jnp.bfloat16))
        left = left - piece
    columns = jnp.concatenate(pieces, axis=1)
    return jnp.pad(columns, ((0, 0), (0, -columns.shape[1] % 128)))


def own_gate(columns, expert, expert_count):
    place = jnp.arange(columns.shape[1], dtype=jnp.int32)
    mine = (place % expert_count == expert) & (place < 3 * expert_count)
    return jnp.sum(jnp.where(mine[None, :], columns.astype(jnp.float32), 0.0), axis=1)[:, None]


def hidden_units(rows, w_gate, w_up):
    gate_value = jnp.dot(rows, w_gate, preferred_element_type=jnp.float32)
    up_value = jnp.dot(rows, w_up, preferred_element_type=jnp.float32)
    return (jax.nn.silu(gate_value) * up_value).astype(jnp.bfloat16)


def body(tokens, routes, gate_weights, w_gate, w_up, w_down):
    devices = lax.axis_size("ep")
    expert_count = devices // 2
    bits = expert_count.bit_length() - 2
    width = tokens.shape[1]
    expert = lax.axis_index("ep") // 2
    columns = gate_columns(routes, gate_weights, expert_count)
    held = gather_rows(jnp.concatenate([tokens, columns], axis=1), bits)
    order = sorted(held, key=lambda mask: mask.bit_count())
    own = jnp.concatenate([held[mask] for mask in order], axis=0)
    other = exchange(own, 1)
    partials = []
    for rows in (other, own):
        hidden = hidden_units(rows[:, :width], w_gate[0], w_up[0])
        value = jnp.dot(hidden, w_down[0], preferred_element_type=jnp.float32)
        partials.append(value * own_gate(rows[:, width:], expert, expert_count))
    arrived = exchange(partials[0].astype(jnp.bfloat16), 1)
    summed = (partials[1] + arrived.astype(jnp.float32)).astype(jnp.bfloat16)
    block = 2 * tokens.shape[0]
    sums = {mask: summed[block * place : block * (place + 1)] for place, mask in enumerate(order)}
    return reduce_rows(sums, bits)


def solution(mesh):
    placed = (
        P(("rep", "ep"), None),
        P(("rep", "ep"), None),
        P(("rep", "ep"), None),
        P("ep", None, None),
        P("ep", None, None),
        P("ep", None, None),
    )
    return jax.shard_map(
        body, mesh=mesh, in_specs=placed, out_specs=P(("rep", "ep"), None), check_vma=False
    )
```

time: 236 us -> 95.7 us (0.41)
  waiting for transfers between devices: 161 us -> 40.3 us
  blocking collectives: 44.3 us -> 0 us
  starting transfers between devices: 0.04 us -> 27.4 us
  between operations: 13.4 us -> 0.17 us
  matrix products: 15.3 us -> 20.4 us
  other arithmetic: 0.26 us -> 4.03 us
    reduce_scatter x1 -> x0, waiting for transfers between devices: 140 us -> none  [body(): return lax.psum_scatter(weighted, 'ep', scatter_dimension=0, tiled=True)]
    all_gather x1 -> x0, blocking collectives: 44.3 us -> none  [body(): all_gates = lax.all_gather(gates, 'ep', axis=0, tiled=True)]
    ppermute x0 -> x20, waiting for transfers between devices: none -> 40.3 us  [exchange(): return lax.ppermute(value, 'ep', pairs)]
    ppermute x0 -> x20, starting transfers between devices: none -> 27.4 us  [exchange(): return lax.ppermute(value, 'ep', pairs)]
    all_gather x1 -> x0, waiting for transfers between devices: 20 us -> none  [body(): rows = lax.all_gather(tokens, 'ep', axis=0, tiled=True)]
    dot_general x2 -> x4, matrix products: 15.3 us -> 20.4 us  [the longest x2 13.6 us: body(): value = jnp.dot(hidden, w_down[0], preferred_element_type=jnp.float32)]
  transfers between devices with their start and end apart: 2 -> 20, of which waited for: 2 -> 16; matrix products, arithmetic and copies ran while one was open for 1% -> 4% of each run, Pallas kernels for 0% -> 0%
where the time goes in v2:
time: 95.7 us; the launch traced here: 95.4 us
  waiting for transfers between devices  40.3 us (42%)
  starting transfers between devices  27.4 us (29%)
  matrix products  20.4 us (21%)
  other arithmetic  4.03 us (4%)
  local copies, waits for them, and re-layouts  3 us (3%)
    ppermute x20, waiting for transfers between devices, exchange(): return lax.ppermute(value, 'ep', pairs)  40.3 us
    ppermute x20, starting transfers between devices, exchange(): return lax.ppermute(value, 'ep', pairs)  27.4 us
    dot_general x2, matrix products, body(): value = jnp.dot(hidden, w_down[0], preferred_element_type=jnp.float32)  13.6 us
    dot_general x2, matrix products, hidden_units(): up_value = jnp.dot(rows, w_up, preferred_element_type=jnp.float32)  6.83 us
    unnamed x14, local copies, waits for them, and re-layouts  2.91 us
  transfers between devices with their start and end apart: 20, of which 16 were waited for; matrix products, arithmetic and copies ran while one was open for 4% of the time, Pallas kernels for 0%

profile of v2, /device:TPU:0, one launch (start us, length us, event | category | flops | bytes accessed | tf_op | source)
XLA Modules:
  0.0 95.4 jit_solution(5274356837488563081)
XLA Ops:
  2.6 4.1 %collective-permute-start = (bf16[16,3712]{1,0:T(8,128)(2,1)S(1)}, bf16[16,3712]{1,0:T(8,128)(2,1)S(1)}, u32[]{:S(2)}, u32[]{:S(2)}) collective-permute-start(bf16[16,3712]{1,0:T(8,128)(2,1)S(1)} %get-tuple-element.16), channel_id=1, source_target_pairs={{0,16},{1,17},{2,18},{3,19},{4,20},{5,21},{6,22},{7,23},{8,24},{9,... | collective-permute-start | bytes 356360 | tf_op jit(solution)/shard_map/ppermute | solution.py:9
  6.8 5.8 %collective-permute-done = bf16[16,3712]{1,0:T(8,128)(2,1)S(1)} collective-permute-done((bf16[16,3712]{1,0:T(8,128)(2,1)S(1)}, bf16[16,3712]{1,0:T(8,128)(2,1)S(1)}, u32[]{:S(2)}, u32[]{:S(2)}) %collective-permute-start) | collective-permute-done | bytes 118816 | tf_op jit(solution)/shard_map/ppermute | solution.py:9
  13.5 1.6 %collective-permute-start.1 = (bf16[32,3712]{1,0:T(8,128)(2,1)S(1)}, bf16[32,3712]{1,0:T(8,128)(2,1)S(1)}, u32[]{:S(2)}, u32[]{:S(2)}) collective-permute-start(bf16[32,3712]{1,0:T(8,128)(2,1)S(1)} %pad_maximum_fusion), channel_id=1, source_target_pairs={{0,2},{1,3},{2,0},{3,1},{4,6},{5,7},{6,4},{7,5},{8,10},{9,11},{10,... | collective-permute-start | bytes 712712 | tf_op jit(solution)/shard_map/ppermute | solution.py:9
  15.1 1.5 %collective-permute-start.2 = (bf16[32,3712]{1,0:T(8,128)(2,1)S(1)}, bf16[32,3712]{1,0:T(8,128)(2,1)S(1)}, u32[]{:S(2)}, u32[]{:S(2)}) collective-permute-start(bf16[32,3712]{1,0:T(8,128)(2,1)S(1)} %pad_maximum_fusion), channel_id=1, source_target_pairs={{0,4},{1,5},{2,6},{3,7},{4,0},{5,1},{6,2},{7,3},{8,12},{9,13},{10,... | collective-permute-start | bytes 712712 | tf_op jit(solution)/shard_map/ppermute | solution.py:9
  17.3 3.2 %collective-permute-done.1 = bf16[32,3712]{1,0:T(8,128)(2,1)S(1)} collective-permute-done((bf16[32,3712]{1,0:T(8,128)(2,1)S(1)}, bf16[32,3712]{1,0:T(8,128)(2,1)S(1)}, u32[]{:S(2)}, u32[]{:S(2)}) %collective-permute-start.1) | collective-permute-done | bytes 237600 | tf_op jit(solution)/shard_map/ppermute | solution.py:9
  20.5 1.5 %collective-permute-start.6 = (bf16[32,3712]{1,0:T(8,128)(2,1)S(1)}, bf16[32,3712]{1,0:T(8,128)(2,1)S(1)}, u32[]{:S(2)}, u32[]{:S(2)}) collective-permute-start(bf16[32,3712]{1,0:T(8,128)(2,1)S(1)} %collective-permute-done.1), channel_id=1, source_target_pairs={{0,8},{1,9},{2,10},{3,11},{4,12},{5,13},{6,14},{7,15},{8,0},{9,1},... | collective-permute-start | bytes 712712 | tf_op jit(solution)/shard_map/ppermute | solution.py:9
  22.0 1.6 %collective-permute-start.4 = (bf16[32,3712]{1,0:T(8,128)(2,1)S(1)}, bf16[32,3712]{1,0:T(8,128)(2,1)S(1)}, u32[]{:S(2)}, u32[]{:S(2)}) collective-permute-start(bf16[32,3712]{1,0:T(8,128)(2,1)S(1)} %collective-permute-done.2), channel_id=1, source_target_pairs={{0,2},{1,3},{2,0},{3,1},{4,6},{5,7},{6,4},{7,5},{8,10},{9,11},{10,... | collective-permute-start | bytes 712712 | tf_op jit(solution)/shard_map/ppermute | solution.py:9
  23.6 1.6 %collective-permute-start.5 = (bf16[32,3712]{1,0:T(8,128)(2,1)S(1)}, bf16[32,3712]{1,0:T(8,128)(2,1)S(1)}, u32[]{:S(2)}, u32[]{:S(2)}) collective-permute-start(bf16[32,3712]{1,0:T(8,128)(2,1)S(1)} %collective-permute-done.3), channel_id=1, source_target_pairs={{0,4},{1,5},{2,6},{3,7},{4,0},{5,1},{6,2},{7,3},{8,12},{9,13},{10,... | collective-permute-start | bytes 712712 | tf_op jit(solution)/shard_map/ppermute | solution.py:9
  25.2 4.7 %collective-permute-done.5 = bf16[32,3712]{1,0:T(8,128)(2,1)S(1)} collective-permute-done((bf16[32,3712]{1,0:T(8,128)(2,1)S(1)}, bf16[32,3712]{1,0:T(8,128)(2,1)S(1)}, u32[]{:S(2)}, u32[]{:S(2)}) %collective-permute-start.5) | collective-permute-done | bytes 237600 | tf_op jit(solution)/shard_map/ppermute | solution.py:9
  30.6 1.6 %collective-permute-start.8 = (bf16[16,3712]{1,0:T(8,128)(2,1)S(1)}, bf16[16,3712]{1,0:T(8,128)(2,1)S(1)}, u32[]{:S(2)}, u32[]{:S(2)}) collective-permute-start(bf16[16,3712]{1,0:T(8,128)(2,1)S(1)} %slice.86), channel_id=1, source_target_pairs={{0,4},{1,5},{2,6},{3,7},{4,0},{5,1},{6,2},{7,3},{8,12},{9,13},{10,... | collective-permute-start | bytes 356360 | tf_op jit(solution)/shard_map/ppermute | solution.py:9
  32.2 2.6 %collective-permute-done.7 = bf16[16,3712]{1,0:T(8,128)(2,1)S(1)} collective-permute-done((bf16[16,3712]{1,0:T(8,128)(2,1)S(1)}, bf16[16,3712]{1,0:T(8,128)(2,1)S(1)}, u32[]{:S(2)}, u32[]{:S(2)}) %collective-permute-start.7) | collective-permute-done | bytes 118816 | tf_op jit(solution)/shard_map/ppermute | solution.py:9
  35.6 4.0 %collective-permute-done.9 = bf16[256,3712]{1,0:T(8,128)(2,1)} collective-permute-done((bf16[256,3712]{1,0:T(8,128)(2,1)S(1)}, bf16[256,3712]{1,0:T(8,128)(2,1)}, u32[]{:S(2)}, u32[]{:S(2)}) %collective-permute-start.9) | collective-permute-done | bytes 1900576 | tf_op jit(solution)/shard_map/ppermute | solution.py:9
  39.6 3.7 %fusion.3 = f32[256,512]{1,0:T(8,128)S(1)} fusion(bf16[1,3584,512]{2,1,0:T(8,128)(2,1)} %param.10, bf16[256,3712]{1,0:T(8,128)(2,1)} %collective-permute-done.9), kind=kOutput, calls=%fused_computation.4 | convolution fusion | flops 939524096 | bytes 6029312 | tf_op jit(solution)/shard_map/dot_general | solution.py:93
  43.3 1.0 %select_reduce_fusion.1 = (f32[256]{0:T(256)S(1)}, f32[256]{0:T(256)S(1)}) fusion(bf16[256,3712]{1,0:T(8,128)(2,1)S(1)} %constant_dynamic-update-slice_fusion, pred[128]{0:T(512)(128)(4,1)S(1)} %compare_and_fusion, bf16[256,3712]{1,0:T(8,128)(2,1)} %collective-permute-done.9), kind=kLoop, calls=%fused_computation.35 | loop fusion | flops 196096 | bytes 133248 | tf_op jit(solution)/shard_map/reduce_sum | solution.py:88
  44.2 7.2 %multiply_convert_fusion = bf16[256,3584]{1,0:T(8,128)(2,1)} fusion(f32[256]{0:T(256)S(1)} %get-tuple-element.6, bf16[1,512,3584]{2,1,0:T(8,128)(2,1)} %param.11, f32[256,512]{1,0:T(8,128)S(1)} %fusion.3, bf16[1,3584,512]{2,1,0:T(8,128)(2,1)} %param.9, bf16[256,3712]{1,0:T(8,128)(2,1)} %collective-permute-done.9), kind=kOutput, calls=%fused_computation.13 | convolution fusion | flops 1881669632 | bytes 11535360 | tf_op jit(solution)/shard_map/dot_general | solution.py:111
  51.5 3.1 %fusion.5 = f32[256,512]{1,0:T(8,128)S(1)} fusion(bf16[1,3584,512]{2,1,0:T(8,128)(2,1)} %param.10, bf16[256,3712]{1,0:T(8,128)(2,1)S(1)} %constant_dynamic-update-slice_fusion), kind=kOutput, calls=%fused_computation.6 | convolution fusion | flops 939524096 | bytes 6029312 | tf_op jit(solution)/shard_map/dot_general | solution.py:93
  55.4 1.2 %copy-done.1 = bf16[256,3584]{1,0:T(8,128)(2,1)} copy-done((bf16[256,3584]{1,0:T(8,128)(2,1)}, bf16[256,3584]{1,0:T(8,128)(2,1)S(1)}, u32[]{:S(2)}) %copy-start.1) | copy-done | bytes 1835032
  56.6 6.4 %add_convert_fusion = bf16[256,3584]{1,0:T(8,128)(2,1)S(1)} fusion(bf16[256,3584]{1,0:T(8,128)(2,1)} %copy-done.1, f32[256]{0:T(256)S(1)} %get-tuple-element.5, bf16[1,512,3584]{2,1,0:T(8,128)(2,1)} %param.11, f32[256,512]{1,0:T(8,128)S(1)} %fusion.5, bf16[1,3584,512]{2,1,0:T(8,128)(2,1)} %param.9, bf16[256,3712]{1,0:T(8,128)(2,1)} %copy-done), kind=kOutput, calls=%fused_computation.12 | convolution fusion | flops 1883504640 | bytes 13370368 | tf_op jit(solution)/shard_map/dot_general | solution.py:111
  63.1 1.6 %collective-permute-start.11 = (bf16[16,3584]{1,0:T(8,128)(2,1)S(1)}, bf16[16,3584]{1,0:T(8,128)(2,1)S(1)}, u32[]{:S(2)}, u32[]{:S(2)}) collective-permute-start(bf16[16,3584]{1,0:T(8,128)(2,1)S(1)} %get-tuple-element.13), channel_id=1, source_target_pairs={{0,4},{1,5},{2,6},{3,7},{4,0},{5,1},{6,2},{7,3},{8,12},{9,13},{10,... | collective-permute-start | bytes 344072 | tf_op jit(solution)/shard_map/ppermute | solution.py:9
  64.7 1.5 %collective-permute-start.16 = (bf16[16,3584]{1,0:T(8,128)(2,1)S(1)}, bf16[16,3584]{1,0:T(8,128)(2,1)S(1)}, u32[]{:S(2)}, u32[]{:S(2)}) collective-permute-start(bf16[16,3584]{1,0:T(8,128)(2,1)S(1)} %get-tuple-element.12), channel_id=1, source_target_pairs={{0,2},{1,3},{2,0},{3,1},{4,6},{5,7},{6,4},{7,5},{8,10},{9,11},{10,... | collective-permute-start | bytes 344072 | tf_op jit(solution)/shard_map/ppermute | solution.py:9
  66.8 1.6 %collective-permute-done.11 = bf16[16,3584]{1,0:T(8,128)(2,1)S(1)} collective-permute-done((bf16[16,3584]{1,0:T(8,128)(2,1)S(1)}, bf16[16,3584]{1,0:T(8,128)(2,1)S(1)}, u32[]{:S(2)}, u32[]{:S(2)}) %collective-permute-start.11) | collective-permute-done | bytes 114720 | tf_op jit(solution)/shard_map/ppermute | solution.py:9
  68.3 2.3 %collective-permute-done.16 = bf16[16,3584]{1,0:T(8,128)(2,1)S(1)} collective-permute-done((bf16[16,3584]{1,0:T(8,128)(2,1)S(1)}, bf16[16,3584]{1,0:T(8,128)(2,1)S(1)}, u32[]{:S(2)}, u32[]{:S(2)}) %collective-permute-start.16) | collective-permute-done | bytes 114720 | tf_op jit(solution)/shard_map/ppermute | solution.py:9
  71.4 1.0 %collective-permute-start.12 = (bf16[32,3584]{1,0:T(8,128)(2,1)S(1)}, bf16[32,3584]{1,0:T(8,128)(2,1)S(1)}, u32[]{:S(2)}, u32[]{:S(2)}) collective-permute-start(bf16[32,3584]{1,0:T(8,128)(2,1)S(1)} %pad_maximum_fusion.1), channel_id=1, source_target_pairs={{0,8},{1,9},{2,10},{3,11},{4,12},{5,13},{6,14},{7,15},{8,0},{9,1},... | collective-permute-start | bytes 688136 | tf_op jit(solution)/shard_map/ppermute | solution.py:9
  72.4 2.1 %collective-permute-done.14 = bf16[32,3584]{1,0:T(8,128)(2,1)S(1)} collective-permute-done((bf16[32,3584]{1,0:T(8,128)(2,1)S(1)}, bf16[32,3584]{1,0:T(8,128)(2,1)S(1)}, u32[]{:S(2)}, u32[]{:S(2)}) %collective-permute-start.14) | collective-permute-done | bytes 229408 | tf_op jit(solution)/shard_map/ppermute | solution.py:9
  74.5 2.4 %collective-permute-done.17 = bf16[32,3584]{1,0:T(8,128)(2,1)S(1)} collective-permute-done((bf16[32,3584]{1,0:T(8,128)(2,1)S(1)}, bf16[32,3584]{1,0:T(8,128)(2,1)S(1)}, u32[]{:S(2)}, u32[]{:S(2)}) %collective-permute-start.17) | collective-permute-done | bytes 229408 | tf_op jit(solution)/shard_map/ppermute | solution.py:9
  77.6 1.6 %collective-permute-start.13 = (bf16[32,3584]{1,0:T(8,128)(2,1)S(1)}, bf16[32,3584]{1,0:T(8,128)(2,1)S(1)}, u32[]{:S(2)}, u32[]{:S(2)}) collective-permute-start(bf16[32,3584]{1,0:T(8,128)(2,1)S(1)} %get-tuple-element.7), channel_id=1, source_target_pairs={{0,2},{1,3},{2,0},{3,1},{4,6},{5,7},{6,4},{7,5},{8,10},{9,11},{10,... | collective-permute-start | bytes 688136 | tf_op jit(solution)/shard_map/ppermute | solution.py:9
  79.2 1.5 %collective-permute-start.15 = (bf16[32,3584]{1,0:T(8,128)(2,1)S(1)}, bf16[32,3584]{1,0:T(8,128)(2,1)S(1)}, u32[]{:S(2)}, u32[]{:S(2)}) collective-permute-start(bf16[32,3584]{1,0:T(8,128)(2,1)S(1)} %get-tuple-element.9), channel_id=1, source_target_pairs={{0,4},{1,5},{2,6},{3,7},{4,0},{5,1},{6,2},{7,3},{8,12},{9,13},{10,... | collective-permute-start | bytes 688136 | tf_op jit(solution)/shard_map/ppermute | solution.py:9
  81.0 2.7 %collective-permute-done.13 = bf16[32,3584]{1,0:T(8,128)(2,1)S(1)} collective-permute-done((bf16[32,3584]{1,0:T(8,128)(2,1)S(1)}, bf16[32,3584]{1,0:T(8,128)(2,1)S(1)}, u32[]{:S(2)}, u32[]{:S(2)}) %collective-permute-start.13) | collective-permute-done | bytes 229408 | tf_op jit(solution)/shard_map/ppermute | solution.py:9
  83.7 1.5 %collective-permute-done.15 = bf16[32,3584]{1,0:T(8,128)(2,1)S(1)} collective-permute-done((bf16[32,3584]{1,0:T(8,128)(2,1)S(1)}, bf16[32,3584]{1,0:T(8,128)(2,1)S(1)}, u32[]{:S(2)}, u32[]{:S(2)}) %collective-permute-start.15) | collective-permute-done | bytes 229408 | tf_op jit(solution)/shard_map/ppermute | solution.py:9
  85.2 1.5 %collective-permute-done.18 = bf16[32,3584]{1,0:T(8,128)(2,1)S(1)} collective-permute-done((bf16[32,3584]{1,0:T(8,128)(2,1)S(1)}, bf16[32,3584]{1,0:T(8,128)(2,1)S(1)}, u32[]{:S(2)}, u32[]{:S(2)}) %collective-permute-start.18) | collective-permute-done | bytes 229408 | tf_op jit(solution)/shard_map/ppermute | solution.py:9
  86.9 3.8 %collective-permute-start.19 = (bf16[16,3584]{1,0:T(8,128)(2,1)S(1)}, bf16[16,3584]{1,0:T(8,128)(2,1)S(1)}, u32[]{:S(2)}, u32[]{:S(2)}) collective-permute-start(bf16[16,3584]{1,0:T(8,128)(2,1)S(1)} %slice.103), channel_id=1, source_target_pairs={{0,16},{1,17},{2,18},{3,19},{4,20},{5,21},{6,22},{7,23},{8,24},{9,... | collective-permute-start | bytes 344072 | tf_op jit(solution)/shard_map/ppermute | solution.py:9
  90.7 4.0 %collective-permute-done.19 = bf16[16,3584]{1,0:T(8,128)(2,1)S(1)} collective-permute-done((bf16[16,3584]{1,0:T(8,128)(2,1)S(1)}, bf16[16,3584]{1,0:T(8,128)(2,1)S(1)}, u32[]{:S(2)}, u32[]{:S(2)}) %collective-permute-start.19) | collective-permute-done | bytes 114720 | tf_op jit(solution)/shard_map/ppermute | solution.py:9
  (45 shorter events, 9.7 us)
Async XLA Ops:
  2.6 9.9 %collective-permute-start = (bf16[16,3712]{1,0:T(8,128)(2,1)S(1)}, bf16[16,3712]{1,0:T(8,128)(2,1)S(1)}, u32[]{:S(2)}, u32[]{:S(2)}) collective-permute-start(bf16[16,3712]{1,0:T(8,128)(2,1)S(1)} %get-tuple-element.16), channel_id=1, source_target_pairs={{0,16},{1,17},{2,18},{3,19},{4,20},{5,21},{6,22},{7,23},{8,24},{9,... | collective-permute-start | bytes 356360 | tf_op jit(solution)/shard_map/ppermute | solution.py:9
  13.5 7.0 %collective-permute-start.1 = (bf16[32,3712]{1,0:T(8,128)(2,1)S(1)}, bf16[32,3712]{1,0:T(8,128)(2,1)S(1)}, u32[]{:S(2)}, u32[]{:S(2)}) collective-permute-start(bf16[32,3712]{1,0:T(8,128)(2,1)S(1)} %pad_maximum_fusion), channel_id=1, source_target_pairs={{0,2},{1,3},{2,0},{3,1},{4,6},{5,7},{6,4},{7,5},{8,10},{9,11},{10,... | collective-permute-start | bytes 712712 | tf_op jit(solution)/shard_map/ppermute | solution.py:9
  15.1 6.9 %collective-permute-start.2 = (bf16[32,3712]{1,0:T(8,128)(2,1)S(1)}, bf16[32,3712]{1,0:T(8,128)(2,1)S(1)}, u32[]{:S(2)}, u32[]{:S(2)}) collective-permute-start(bf16[32,3712]{1,0:T(8,128)(2,1)S(1)} %pad_maximum_fusion), channel_id=1, source_target_pairs={{0,4},{1,5},{2,6},{3,7},{4,0},{5,1},{6,2},{7,3},{8,12},{9,13},{10,... | collective-permute-start | bytes 712712 | tf_op jit(solution)/shard_map/ppermute | solution.py:9
  16.6 7.0 %collective-permute-start.3 = (bf16[32,3712]{1,0:T(8,128)(2,1)S(1)}, bf16[32,3712]{1,0:T(8,128)(2,1)S(1)}, u32[]{:S(2)}, u32[]{:S(2)}) collective-permute-start(bf16[32,3712]{1,0:T(8,128)(2,1)S(1)} %pad_maximum_fusion), channel_id=1, source_target_pairs={{0,8},{1,9},{2,10},{3,11},{4,12},{5,13},{6,14},{7,15},{8,0},{9,1},... | collective-permute-start | bytes 712712 | tf_op jit(solution)/shard_map/ppermute | solution.py:9
  20.5 10.1 %collective-permute-start.6 = (bf16[32,3712]{1,0:T(8,128)(2,1)S(1)}, bf16[32,3712]{1,0:T(8,128)(2,1)S(1)}, u32[]{:S(2)}, u32[]{:S(2)}) collective-permute-start(bf16[32,3712]{1,0:T(8,128)(2,1)S(1)} %collective-permute-done.1), channel_id=1, source_target_pairs={{0,8},{1,9},{2,10},{3,11},{4,12},{5,13},{6,14},{7,15},{8,0},{9,1},... | collective-permute-start | bytes 712712 | tf_op jit(solution)/shard_map/ppermute | solution.py:9
  22.0 10.2 %collective-permute-start.4 = (bf16[32,3712]{1,0:T(8,128)(2,1)S(1)}, bf16[32,3712]{1,0:T(8,128)(2,1)S(1)}, u32[]{:S(2)}, u32[]{:S(2)}) collective-permute-start(bf16[32,3712]{1,0:T(8,128)(2,1)S(1)} %collective-permute-done.2), channel_id=1, source_target_pairs={{0,2},{1,3},{2,0},{3,1},{4,6},{5,7},{6,4},{7,5},{8,10},{9,11},{10,... | collective-permute-start | bytes 712712 | tf_op jit(solution)/shard_map/ppermute | solution.py:9
  23.6 6.4 %collective-permute-start.5 = (bf16[32,3712]{1,0:T(8,128)(2,1)S(1)}, bf16[32,3712]{1,0:T(8,128)(2,1)S(1)}, u32[]{:S(2)}, u32[]{:S(2)}) collective-permute-start(bf16[32,3712]{1,0:T(8,128)(2,1)S(1)} %collective-permute-done.3), channel_id=1, source_target_pairs={{0,4},{1,5},{2,6},{3,7},{4,0},{5,1},{6,2},{7,3},{8,12},{9,13},{10,... | collective-permute-start | bytes 712712 | tf_op jit(solution)/shard_map/ppermute | solution.py:9
  29.9 4.9 %collective-permute-start.7 = (bf16[16,3712]{1,0:T(8,128)(2,1)S(1)}, bf16[16,3712]{1,0:T(8,128)(2,1)S(1)}, u32[]{:S(2)}, u32[]{:S(2)}) collective-permute-start(bf16[16,3712]{1,0:T(8,128)(2,1)S(1)} %slice.85), channel_id=1, source_target_pairs={{0,2},{1,3},{2,0},{3,1},{4,6},{5,7},{6,4},{7,5},{8,10},{9,11},{10,... | collective-permute-start | bytes 356360 | tf_op jit(solution)/shard_map/ppermute | solution.py:9
  30.6 4.9 %collective-permute-start.8 = (bf16[16,3712]{1,0:T(8,128)(2,1)S(1)}, bf16[16,3712]{1,0:T(8,128)(2,1)S(1)}, u32[]{:S(2)}, u32[]{:S(2)}) collective-permute-start(bf16[16,3712]{1,0:T(8,128)(2,1)S(1)} %slice.86), channel_id=1, source_target_pairs={{0,4},{1,5},{2,6},{3,7},{4,0},{5,1},{6,2},{7,3},{8,12},{9,13},{10,... | collective-permute-start | bytes 356360 | tf_op jit(solution)/shard_map/ppermute | solution.py:9
  35.5 16.1 %copy-start = (bf16[256,3712]{1,0:T(8,128)(2,1)}, bf16[256,3712]{1,0:T(8,128)(2,1)S(1)}, u32[]{:S(2)}) copy-start(bf16[256,3712]{1,0:T(8,128)(2,1)S(1)} %constant_dynamic-update-slice_fusion) | copy-start | bytes 5701636
  35.5 4.1 %collective-permute-start.9 = (bf16[256,3712]{1,0:T(8,128)(2,1)S(1)}, bf16[256,3712]{1,0:T(8,128)(2,1)}, u32[]{:S(2)}, u32[]{:S(2)}) collective-permute-start(bf16[256,3712]{1,0:T(8,128)(2,1)S(1)} %constant_dynamic-update-slice_fusion), channel_id=1, source_target_pairs={{0,1},{1,0},{2,3},{3,2},{4,5},{5,4},{6,7},{7,6},{8,9},{9,8},{10,11... | collective-permute-start | bytes 5701640 | tf_op jit(solution)/shard_map/ppermute | solution.py:9
  51.4 4.0 %collective-permute-start.10 = (bf16[256,3584]{1,0:T(8,128)(2,1)}, bf16[256,3584]{1,0:T(8,128)(2,1)S(1)}, u32[]{:S(2)}, u32[]{:S(2)}) collective-permute-start(bf16[256,3584]{1,0:T(8,128)(2,1)} %multiply_convert_fusion), channel_id=1, source_target_pairs={{0,1},{1,0},{2,3},{3,2},{4,5},{5,4},{6,7},{7,6},{8,9},{9,8},{10,11... | collective-permute-start | bytes 5505032 | tf_op jit(solution)/shard_map/ppermute | solution.py:9
  55.4 1.2 %copy-start.1 = (bf16[256,3584]{1,0:T(8,128)(2,1)}, bf16[256,3584]{1,0:T(8,128)(2,1)S(1)}, u32[]{:S(2)}) copy-start(bf16[256,3584]{1,0:T(8,128)(2,1)S(1)} %collective-permute-done.10) | copy-start | bytes 5505028
  63.1 5.3 %collective-permute-start.11 = (bf16[16,3584]{1,0:T(8,128)(2,1)S(1)}, bf16[16,3584]{1,0:T(8,128)(2,1)S(1)}, u32[]{:S(2)}, u32[]{:S(2)}) collective-permute-start(bf16[16,3584]{1,0:T(8,128)(2,1)S(1)} %get-tuple-element.13), channel_id=1, source_target_pairs={{0,4},{1,5},{2,6},{3,7},{4,0},{5,1},{6,2},{7,3},{8,12},{9,13},{10,... | collective-permute-start | bytes 344072 | tf_op jit(solution)/shard_map/ppermute | solution.py:9
  64.7 6.0 %collective-permute-start.16 = (bf16[16,3584]{1,0:T(8,128)(2,1)S(1)}, bf16[16,3584]{1,0:T(8,128)(2,1)S(1)}, u32[]{:S(2)}, u32[]{:S(2)}) collective-permute-start(bf16[16,3584]{1,0:T(8,128)(2,1)S(1)} %get-tuple-element.12), channel_id=1, source_target_pairs={{0,2},{1,3},{2,0},{3,1},{4,6},{5,7},{6,4},{7,5},{8,10},{9,11},{10,... | collective-permute-start | bytes 344072 | tf_op jit(solution)/shard_map/ppermute | solution.py:9
  66.2 8.3 %collective-permute-start.14 = (bf16[32,3584]{1,0:T(8,128)(2,1)S(1)}, bf16[32,3584]{1,0:T(8,128)(2,1)S(1)}, u32[]{:S(2)}, u32[]{:S(2)}) collective-permute-start(bf16[32,3584]{1,0:T(8,128)(2,1)S(1)} %slice.97), channel_id=1, source_target_pairs={{0,2},{1,3},{2,0},{3,1},{4,6},{5,7},{6,4},{7,5},{8,10},{9,11},{10,... | collective-permute-start | bytes 688136 | tf_op jit(solution)/shard_map/ppermute | solution.py:9
  70.8 6.1 %collective-permute-start.17 = (bf16[32,3584]{1,0:T(8,128)(2,1)S(1)}, bf16[32,3584]{1,0:T(8,128)(2,1)S(1)}, u32[]{:S(2)}, u32[]{:S(2)}) collective-permute-start(bf16[32,3584]{1,0:T(8,128)(2,1)S(1)} %pad_maximum_fusion.2), channel_id=1, source_target_pairs={{0,4},{1,5},{2,6},{3,7},{4,0},{5,1},{6,2},{7,3},{8,12},{9,13},{10,... | collective-permute-start | bytes 688136 | tf_op jit(solution)/shard_map/ppermute | solution.py:9
  71.4 6.1 %collective-permute-start.12 = (bf16[32,3584]{1,0:T(8,128)(2,1)S(1)}, bf16[32,3584]{1,0:T(8,128)(2,1)S(1)}, u32[]{:S(2)}, u32[]{:S(2)}) collective-permute-start(bf16[32,3584]{1,0:T(8,128)(2,1)S(1)} %pad_maximum_fusion.1), channel_id=1, source_target_pairs={{0,8},{1,9},{2,10},{3,11},{4,12},{5,13},{6,14},{7,15},{8,0},{9,1},... | collective-permute-start | bytes 688136 | tf_op jit(solution)/shard_map/ppermute | solution.py:9
  77.6 6.1 %collective-permute-start.13 = (bf16[32,3584]{1,0:T(8,128)(2,1)S(1)}, bf16[32,3584]{1,0:T(8,128)(2,1)S(1)}, u32[]{:S(2)}, u32[]{:S(2)}) collective-permute-start(bf16[32,3584]{1,0:T(8,128)(2,1)S(1)} %get-tuple-element.7), channel_id=1, source_target_pairs={{0,2},{1,3},{2,0},{3,1},{4,6},{5,7},{6,4},{7,5},{8,10},{9,11},{10,... | collective-permute-start | bytes 688136 | tf_op jit(solution)/shard_map/ppermute | solution.py:9
  79.2 6.0 %collective-permute-start.15 = (bf16[32,3584]{1,0:T(8,128)(2,1)S(1)}, bf16[32,3584]{1,0:T(8,128)(2,1)S(1)}, u32[]{:S(2)}, u32[]{:S(2)}) collective-permute-start(bf16[32,3584]{1,0:T(8,128)(2,1)S(1)} %get-tuple-element.9), channel_id=1, source_target_pairs={{0,4},{1,5},{2,6},{3,7},{4,0},{5,1},{6,2},{7,3},{8,12},{9,13},{10,... | collective-permute-start | bytes 688136 | tf_op jit(solution)/shard_map/ppermute | solution.py:9
  80.7 6.0 %collective-permute-start.18 = (bf16[32,3584]{1,0:T(8,128)(2,1)S(1)}, bf16[32,3584]{1,0:T(8,128)(2,1)S(1)}, u32[]{:S(2)}, u32[]{:S(2)}) collective-permute-start(bf16[32,3584]{1,0:T(8,128)(2,1)S(1)} %get-tuple-element.8), channel_id=1, source_target_pairs={{0,8},{1,9},{2,10},{3,11},{4,12},{5,13},{6,14},{7,15},{8,0},{9,1},... | collective-permute-start | bytes 688136 | tf_op jit(solution)/shard_map/ppermute | solution.py:9
  86.9 7.8 %collective-permute-start.19 = (bf16[16,3584]{1,0:T(8,128)(2,1)S(1)}, bf16[16,3584]{1,0:T(8,128)(2,1)S(1)}, u32[]{:S(2)}, u32[]{:S(2)}) collective-permute-start(bf16[16,3584]{1,0:T(8,128)(2,1)S(1)} %slice.103), channel_id=1, source_target_pairs={{0,16},{1,17},{2,18},{3,19},{4,20},{5,21},{6,22},{7,23},{8,24},{9,... | collective-permute-start | bytes 344072 | tf_op jit(solution)/shard_map/ppermute | solution.py:9
